TPU v7x, 32 devices: a whole 2x2x4 slice. The times are simulated.
32 devices in a mesh: lon: 8 (over z, x), lat: 4 (over y, core).
Axes of the slice: x: 2, y: 2, z: 4, core: 2. Of those that a mesh axis runs over, the one named last changes fastest.
Arguments:
- efield_north: float32 [128, 3072], P('lat', 'lon'), may hold values from -13 to 14
- efield_east: float32 [128, 3072], P('lat', 'lon'), may hold values from -13 to 14
- efield_up: float32 [128, 3072], P('lat', 'lon'), may hold values from -13 to 14
- hfield_north: float32 [128, 3072], P('lat', 'lon'), may hold values from -13 to 14
- hfield_east: float32 [128, 3072], P('lat', 'lon'), may hold values from -13 to 14
- hfield_up: float32 [128, 3072], P('lat', 'lon'), may hold values from -13 to 14
- sigma_profile: float32 [24], replicated, may hold values from 0.001 to 30
- flash_lat: int32 [64], replicated, may hold values from 0 to 126
- flash_lon: int32 [64], replicated, may hold values from 0 to 127
- flash_step: int32 [64], replicated, may hold values from 0 to 8
- flash_amp: float32 [64], replicated, may hold values from 20 to 60
Outputs:
- electric_north: float32 [128, 3072], P('lat', 'lon')
- electric_east: float32 [128, 3072], P('lat', 'lon')
- electric_up: float32 [128, 3072], P('lat', 'lon')
- magnetic_north: float32 [128, 3072], P('lat', 'lon')
- magnetic_east: float32 [128, 3072], P('lat', 'lon')
- magnetic_up: float32 [128, 3072], P('lat', 'lon')
- zonal_means: float32 [9, 2, 128, 24], P(None, None, 'lat')
All inputs are finite; a program needn't handle non-finite values.
Results may differ from a plain program's by a relative error of at most 0.0003.
Values sent between devices are 32-bit elements; how exact they have to be, the bound alone decides.
A program may use at most 64 MiB of HBM per device.

v0:
```python
import math

import jax
import jax.numpy as jnp
from jax import lax
from jax.sharding import PartitionSpec as P

CHANNEL = 3
STEPS = 9


RADIUS_CELLS = 1529.0
COURANT = 0.9


def shifted_2(x, axis, by):
    size = lax.axis_size(axis)
    return lax.ppermute(x, axis, [(i, (i + by) % size) for i in range(size)])


def shifted_3(value, axis, steps):
    count = lax.axis_size(axis)
    initial, last = (max(0, -steps), min(count, count - steps))
    return lax.ppermute(value, axis, [(source, source + steps) for source in range(initial, last)])


def time_step(lat_count, lon_count):
    lon_angle = 2.0 * math.pi / lon_count
    lat_angle = math.pi / lat_count
    narrowest = RADIUS_CELLS * lon_angle * math.sin(lat_angle)
    lat_length = RADIUS_CELLS * lat_angle
    return COURANT / math.sqrt(1.0 / narrowest**2 + 1.0 / lat_length**2 + 1.0)


def grid_terms(row_index, lat_count, lon_count):
    lon_angle = 2.0 * math.pi / lon_count
    lat_angle = math.pi / lat_count
    row_place = row_index.astype(jnp.float32)
    centre = -0.5 * math.pi + (row_place + 0.5) * lat_angle
    north_edge = centre + 0.5 * lat_angle
    south_edge = centre - 0.5 * lat_angle
    next_centre = centre + lat_angle
    at_pole = row_index == lat_count - 1
    at_south = row_index == 0
    scale_lon = RADIUS_CELLS * lon_angle
    band_area = 2.0 * RADIUS_CELLS * scale_lon * math.sin(0.5 * lat_angle)
    span_centre = scale_lon * jnp.cos(centre)
    span_next = scale_lon * jnp.cos(next_centre)
    span_edge = jnp.where(at_pole, 0.0, scale_lon * jnp.cos(north_edge))
    span_south = jnp.where(at_south, 0.0, scale_lon * jnp.cos(south_edge))
    area_centre = band_area * jnp.cos(centre)
    area_edge = jnp.where(at_pole, 1.0, band_area * jnp.cos(north_edge))
    safe_edge = jnp.where(at_pole, 1.0, span_edge)
    keeper = jnp.where(at_pole, 0.0, 1.0)
    return (
        span_centre,
        span_next,
        span_edge,
        span_south,
        area_centre,
        area_edge,
        safe_edge,
        keeper,
    )


def level_above(values, top_mask):
    shifted = jnp.concatenate([values[:, 1:], jnp.zeros_like(values[:, :1])], axis=1)
    return jnp.where(top_mask, shifted, 0.0)


def level_below(values, bottom_mask):
    shifted = jnp.concatenate([jnp.zeros_like(values[:, :1]), values[:, :-1]], axis=1)
    return jnp.where(bottom_mask, shifted, 0.0)


def zonal_fold(values, lat_rows, lon_cols, layers):
    return jnp.sum(values.reshape(lat_rows, lon_cols, layers), axis=1)


def body(
    efield_north,
    efield_east,
    efield_up,
    hfield_north,
    hfield_east,
    hfield_up,
    sigma_profile,
    flash_lat,
    flash_lon,
    flash_step,
    flash_amp,
):
    lat_rows, own_lanes = efield_north.shape
    layers = sigma_profile.shape[0]
    lon_cols = own_lanes // layers
    lat_count = lat_rows * lax.axis_size("lat")
    lon_count = lon_cols * lax.axis_size("lon")
    time_delta = time_step(lat_count, lon_count)
    lat_length = RADIUS_CELLS * math.pi / lat_count
    half_loss = 0.5 * time_delta * sigma_profile
    decay_layer = (1.0 - half_loss) / (1.0 + half_loss)
    drive_layer = time_delta / (1.0 + half_loss)
    channel_layer = (jnp.arange(layers) < CHANNEL).astype(jnp.float32)
    margin = 0
    row_count = lat_rows + 2 * margin
    cell_count = lon_cols + 2 * margin
    lane_count = cell_count * layers
    row_index = lax.axis_index("lat") * lat_rows - margin + jnp.arange(row_count, dtype=jnp.int32)
    cell_index = (
        lax.axis_index("lon") * lon_cols - margin + jnp.arange(cell_count, dtype=jnp.int32)
    ) % lon_count
    clipped = jnp.clip(row_index, 0, lat_count - 1)
    metric_terms = [
        metric_term[:, None] for metric_term in grid_terms(clipped, lat_count, lon_count)
    ]
    span_centre, span_next, span_edge, span_south, area_centre, area_edge, safe_edge, keeper = (
        metric_terms
    )
    south_row = (row_index == 0)[:, None]
    north_row = (row_index == lat_count - 1)[:, None]
    layer_of_lane = jnp.arange(lane_count, dtype=jnp.int32) % layers
    top_mask = (layer_of_lane != layers - 1)[None, :]
    bottom_mask = (layer_of_lane != 0)[None, :]
    decay_lane = jnp.tile(decay_layer, cell_count)[None, :]
    drive_lane = jnp.tile(drive_layer, cell_count)[None, :]
    lane_cell = jnp.repeat(cell_index, layers)
    lon_table = (flash_lon[:, None] == lane_cell[None, :]).astype(jnp.float32) * (
        drive_lane * jnp.tile(channel_layer, cell_count)[None, :]
    )
    lat_onehot = (flash_lat[:, None] == row_index[None, :]).astype(jnp.float32)
    cap_index = jnp.array([0, lat_count - 2, lat_count - 1], dtype=jnp.int32)
    cap_metric = grid_terms(cap_index, lat_count, lon_count)
    e_north = efield_north
    e_east = keeper * efield_east
    e_up = keeper * efield_up
    h_north = keeper * hfield_north
    h_east = hfield_east
    h_up = hfield_up
    history = []
    for step_index in range(STEPS):
        inner_east = e_east
        inner_up = h_up
        local_sums = jnp.stack(
            [
                zonal_fold(inner_east, lat_rows, lon_cols, layers),
                zonal_fold(inner_up, lat_rows, lon_cols, layers),
            ]
        )
        history.append(local_sums)
        cap_rows = jnp.stack(
            [
                local_sums[0, 0],
                local_sums[0, lat_rows - 2],
                local_sums[1, 0],
                local_sums[1, lat_rows - 1],
            ]
        )
        cap_means = lax.psum(cap_rows, "lon") / lon_count
        south_cap = cap_means[2] + time_delta * cap_metric[2][0] * cap_means[0] / cap_metric[4][0]
        north_cap = cap_means[3] - time_delta * cap_metric[2][1] * cap_means[1] / cap_metric[4][2]
        south_cap, north_cap = (
            jnp.tile(south_cap, cell_count)[None, :],
            jnp.tile(north_cap, cell_count)[None, :],
        )
        east_face = shifted_2(
            jnp.concatenate([e_north[:, :layers], e_up[:, :layers]], axis=1), "lon", -1
        )
        south_face = shifted_3(jnp.concatenate([e_east[-1:], e_up[-1:]], axis=0), "lat", 1)
        north_next = jnp.concatenate([e_north[:, layers:], east_face[:, :layers]], axis=1)
        up_next = jnp.concatenate([e_up[:, layers:], east_face[:, layers:]], axis=1)
        east_south = jnp.concatenate([south_face[0:1], e_east[:-1]], axis=0)
        up_south = jnp.concatenate([south_face[1:2], e_up[:-1]], axis=0)
        circulation = (
            span_south * east_south - span_edge * e_east + lat_length * (north_next - e_north)
        )
        up_new = h_up - time_delta * circulation / area_centre
        up_new = jnp.where(south_row, south_cap, up_new)
        up_new = jnp.where(north_row, north_cap, up_new)
        north_new = keeper * (
            h_north
            - time_delta * ((e_up - up_next) / safe_edge + level_above(e_east, top_mask) - e_east)
        )
        east_new = h_east - time_delta * (
            (e_up - up_south) / lat_length - (level_above(e_north, top_mask) - e_north)
        )
        h_up, h_north, h_east = (up_new, north_new, east_new)
        west_face = shifted_2(
            jnp.concatenate([h_up[:, -layers:], h_north[:, -layers:]], axis=1), "lon", 1
        )
        north_face = shifted_3(jnp.concatenate([h_up[:1], h_east[:1]], axis=0), "lat", -1)
        up_west = jnp.concatenate([west_face[:, :layers], h_up[:, :-layers]], axis=1)
        hnorth_west = jnp.concatenate([west_face[:, layers:], h_north[:, :-layers]], axis=1)
        up_north = jnp.concatenate([h_up[1:], north_face[0:1]], axis=0)
        heast_north = jnp.concatenate([h_east[1:], north_face[1:2]], axis=0)
        e_north_new = decay_lane * e_north + drive_lane * (
            h_east - level_below(h_east, bottom_mask) - (h_up - up_west) / span_centre
        )
        e_east_new = keeper * (
            decay_lane * e_east
            + drive_lane
            * ((up_north - h_up) / lat_length - (h_north - level_below(h_north, bottom_mask)))
        )
        loop_flux = (
            span_centre * h_east - span_next * heast_north + lat_length * (h_north - hnorth_west)
        )
        strike = (flash_step == step_index).astype(jnp.float32) * flash_amp
        weighted = lat_onehot * strike[:, None]
        source = lax.dot_general(
            weighted,
            lon_table,
            (((0,), (0,)), ((), ())),
            precision=lax.Precision.HIGHEST,
            preferred_element_type=jnp.float32,
        )
        e_up_new = keeper * (decay_lane * e_up + drive_lane * loop_flux / area_edge) + source
        e_north, e_east, e_up = (e_north_new, e_east_new, e_up_new)
    zonal_out = lax.psum(jnp.stack(history), "lon") / lon_count
    return (e_north, e_east, e_up, h_north, h_east, h_up, zonal_out)


def solution(mesh):
    in_specs = (
        P("lat", "lon"),
        P("lat", "lon"),
        P("lat", "lon"),
        P("lat", "lon"),
        P("lat", "lon"),
        P("lat", "lon"),
        P(),
        P(),
        P(),
        P(),
        P(),
    )
    out_specs = (
        P("lat", "lon"),
        P("lat", "lon"),
        P("lat", "lon"),
        P("lat", "lon"),
        P("lat", "lon"),
        P("lat", "lon"),
        P(None, None, "lat", None),
    )
    return jax.shard_map(body, mesh=mesh, in_specs=in_specs, out_specs=out_specs, check_vma=False)
```

profile of v0, /device:TPU:0, one launch (start us, length us, event | category | flops | bytes accessed | tf_op | source)
XLA Modules:
  0.0 314.3 jit_solution(11947117008634224123)
XLA Ops:
  0.7 0.9 broadcast_multiply_fusion.1
  1.6 2.4 collective-permute-start
  4.8 5.4 %collective-permute-start.1 = (f32[32,48]{1,0:T(8,128)S(1)}, f32[32,48]{1,0:T(8,128)S(1)}, u32[]{:S(2)}, u32[]{:S(2)}) collective-permute-start(f32[32,48]{1,0:T(8,128)S(1)} %pad_maximum_fusion), channel_id=1, source_target_pairs={{0,28},{4,0},{8,4},{12,8},{16,12},{20,16},{24,20},{28,24},{1,29},{... | collective-permute-start | bytes 18440 | tf_op jit(solution)/shard_map/ppermute | solution.py:18
  11.3 17.7 %psum.70 = f32[4,24]{1,0:T(4,128)S(1)} all-reduce(f32[4,24]{1,0:T(4,128)S(1)} %pad_maximum_fusion.36), channel_id=1, replica_groups=mesh['lon'=8,'lat'=4] {'lon'}, use_global_device_ids=true, to_apply=%region_2.3 | all-reduce | flops 96 | bytes 768 | tf_op jit(solution)/shard_map/psum | solution.py:159
  32.6 1.3 collective-permute-start.3
  34.0 1.5 collective-permute-start.2
  35.6 4.9 %collective-permute-done.2 = f32[32,48]{1,0:T(8,128)S(1)} collective-permute-done((f32[32,48]{1,0:T(8,128)S(1)}, f32[32,48]{1,0:T(8,128)S(1)}, u32[]{:S(2)}, u32[]{:S(2)}) %collective-permute-start.2) | collective-permute-done | bytes 6176 | tf_op jit(solution)/shard_map/ppermute | solution.py:18
  42.3 2.0 collective-permute-start.4
  44.5 19.1 %psum.71 = f32[4,24]{1,0:T(4,128)S(1)} all-reduce(f32[4,24]{1,0:T(4,128)S(1)} %pad_maximum_fusion.37), channel_id=1, replica_groups=mesh['lon'=8,'lat'=4] {'lon'}, use_global_device_ids=true, to_apply=%region_5.6 | all-reduce | flops 96 | bytes 768 | tf_op jit(solution)/shard_map/psum | solution.py:159
  64.5 1.3 collective-permute-start.7
  66.0 1.5 collective-permute-done.7
  67.6 4.9 %collective-permute-done.6 = f32[32,48]{1,0:T(8,128)S(1)} collective-permute-done((f32[32,48]{1,0:T(8,128)S(1)}, f32[32,48]{1,0:T(8,128)S(1)}, u32[]{:S(2)}, u32[]{:S(2)}) %collective-permute-start.6) | collective-permute-done | bytes 6176 | tf_op jit(solution)/shard_map/ppermute | solution.py:18
  73.6 2.0 collective-permute-start.8
  75.8 19.1 %psum.72 = f32[4,24]{1,0:T(4,128)S(1)} all-reduce(f32[4,24]{1,0:T(4,128)S(1)} %pad_maximum_fusion.38), channel_id=1, replica_groups=mesh['lon'=8,'lat'=4] {'lon'}, use_global_device_ids=true, to_apply=%region_8.9 | all-reduce | flops 96 | bytes 768 | tf_op jit(solution)/shard_map/psum | solution.py:159
  95.8 1.3 collective-permute-start.11
  97.3 1.5 collective-permute-done.11
  98.8 4.9 %collective-permute-done.10 = f32[32,48]{1,0:T(8,128)S(1)} collective-permute-done((f32[32,48]{1,0:T(8,128)S(1)}, f32[32,48]{1,0:T(8,128)S(1)}, u32[]{:S(2)}, u32[]{:S(2)}) %collective-permute-start.10) | collective-permute-done | bytes 6176 | tf_op jit(solution)/shard_map/ppermute | solution.py:18
  104.8 2.0 collective-permute-start.12
  107.0 19.1 %psum.73 = f32[4,24]{1,0:T(4,128)S(1)} all-reduce(f32[4,24]{1,0:T(4,128)S(1)} %pad_maximum_fusion.39), channel_id=1, replica_groups=mesh['lon'=8,'lat'=4] {'lon'}, use_global_device_ids=true, to_apply=%region_11.12 | all-reduce | flops 96 | bytes 768 | tf_op jit(solution)/shard_map/psum | solution.py:159
  127.0 1.3 collective-permute-start.15
  128.6 1.5 collective-permute-done.15
  130.1 4.9 %collective-permute-done.14 = f32[32,48]{1,0:T(8,128)S(1)} collective-permute-done((f32[32,48]{1,0:T(8,128)S(1)}, f32[32,48]{1,0:T(8,128)S(1)}, u32[]{:S(2)}, u32[]{:S(2)}) %collective-permute-start.14) | collective-permute-done | bytes 6176 | tf_op jit(solution)/shard_map/ppermute | solution.py:18
  136.1 2.0 collective-permute-start.16
  138.3 19.2 %psum.74 = f32[4,24]{1,0:T(4,128)S(1)} all-reduce(f32[4,24]{1,0:T(4,128)S(1)} %pad_maximum_fusion.40), channel_id=1, replica_groups=mesh['lon'=8,'lat'=4] {'lon'}, use_global_device_ids=true, to_apply=%region_14.15 | all-reduce | flops 96 | bytes 768 | tf_op jit(solution)/shard_map/psum | solution.py:159
  158.3 1.3 collective-permute-start.19
  159.9 1.5 collective-permute-done.19
  161.4 4.9 %collective-permute-done.18 = f32[32,48]{1,0:T(8,128)S(1)} collective-permute-done((f32[32,48]{1,0:T(8,128)S(1)}, f32[32,48]{1,0:T(8,128)S(1)}, u32[]{:S(2)}, u32[]{:S(2)}) %collective-permute-start.18) | collective-permute-done | bytes 6176 | tf_op jit(solution)/shard_map/ppermute | solution.py:18
  167.4 2.0 collective-permute-start.20
  169.6 19.1 %psum.75 = f32[4,24]{1,0:T(4,128)S(1)} all-reduce(f32[4,24]{1,0:T(4,128)S(1)} %pad_maximum_fusion.41), channel_id=1, replica_groups=mesh['lon'=8,'lat'=4] {'lon'}, use_global_device_ids=true, to_apply=%region_17.18 | all-reduce | flops 96 | bytes 768 | tf_op jit(solution)/shard_map/psum | solution.py:159
  189.6 1.3 collective-permute-start.23
  191.1 1.5 collective-permute-done.23
  192.7 4.9 %collective-permute-done.22 = f32[32,48]{1,0:T(8,128)S(1)} collective-permute-done((f32[32,48]{1,0:T(8,128)S(1)}, f32[32,48]{1,0:T(8,128)S(1)}, u32[]{:S(2)}, u32[]{:S(2)}) %collective-permute-start.22) | collective-permute-done | bytes 6176 | tf_op jit(solution)/shard_map/ppermute | solution.py:18
  198.7 2.0 collective-permute-start.24
  200.9 19.1 %psum.76 = f32[4,24]{1,0:T(4,128)S(1)} all-reduce(f32[4,24]{1,0:T(4,128)S(1)} %pad_maximum_fusion.42), channel_id=1, replica_groups=mesh['lon'=8,'lat'=4] {'lon'}, use_global_device_ids=true, to_apply=%region_20.21 | all-reduce | flops 96 | bytes 768 | tf_op jit(solution)/shard_map/psum | solution.py:159
  220.9 1.3 collective-permute-start.27
  222.4 1.8 collective-permute-done.27
  224.2 4.6 %collective-permute-done.26 = f32[32,48]{1,0:T(8,128)S(1)} collective-permute-done((f32[32,48]{1,0:T(8,128)S(1)}, f32[32,48]{1,0:T(8,128)S(1)}, u32[]{:S(2)}, u32[]{:S(2)}) %collective-permute-start.26) | collective-permute-done | bytes 6176 | tf_op jit(solution)/shard_map/ppermute | solution.py:18
  229.9 2.2 collective-permute-start.28
  232.3 19.3 %psum.77 = f32[4,24]{1,0:T(4,128)S(1)} all-reduce(f32[4,24]{1,0:T(4,128)S(1)} %pad_maximum_fusion.43), channel_id=1, replica_groups=mesh['lon'=8,'lat'=4] {'lon'}, use_global_device_ids=true, to_apply=%region_23.24 | all-reduce | flops 96 | bytes 768 | tf_op jit(solution)/shard_map/psum | solution.py:159
  252.5 1.3 collective-permute-start.31
  254.1 2.1 collective-permute-done.31
  256.2 4.2 %collective-permute-done.30 = f32[32,48]{1,0:T(8,128)S(1)} collective-permute-done((f32[32,48]{1,0:T(8,128)S(1)}, f32[32,48]{1,0:T(8,128)S(1)}, u32[]{:S(2)}, u32[]{:S(2)}) %collective-permute-start.30) | collective-permute-done | bytes 6176 | tf_op jit(solution)/shard_map/ppermute | solution.py:18
  261.4 2.5 collective-permute-start.32
  264.2 38.8 %all-reduce.36 = (f32[4,24]{1,0:T(4,128)S(1)}, f32[9,2,32,24]{3,2,1,0:T(8,128)S(1)}) all-reduce(f32[4,24]{1,0:T(4,128)S(1)} %pad_maximum_fusion.44, f32[9,2,32,24]{3,2,1,0:T(8,128)S(1)} %fusion.368), channel_id=1, replica_groups=mesh['lon'=8,'lat'=4] {'lon'}, use_global_device_ids=true, to_apply=%region_26.27 | all-reduce | flops 13920 | bytes 111360 | tf_op jit(solution)/shard_map/psum | solution.py:159
  304.7 1.3 collective-permute-start.35
  306.1 1.6 collective-permute-done.35
  307.7 4.8 %collective-permute-done.34 = f32[32,48]{1,0:T(8,128)S(1)} collective-permute-done((f32[32,48]{1,0:T(8,128)S(1)}, f32[32,48]{1,0:T(8,128)S(1)}, u32[]{:S(2)}, u32[]{:S(2)}) %collective-permute-start.34) | collective-permute-done | bytes 6176 | tf_op jit(solution)/shard_map/ppermute | solution.py:18
  312.6 0.9 convolution_add_fusion
  (442 shorter events, 25.2 us)
Async XLA Ops:
  1.6 29.7 %collective-permute-start = (f32[2,384]{1,0:T(2,128)S(1)}, f32[2,384]{1,0:T(2,128)S(1)}, u32[]{:S(2)}, u32[]{:S(2)}) collective-permute-start(f32[2,384]{1,0:T(2,128)S(1)} %pad_maximum_fusion.18), channel_id=1, source_target_pairs={{0,1},{1,2},{2,3},{4,5},{5,6},{6,7},{8,9},{9,10},{10,11},{12,13},{... | collective-permute-start | bytes 9224 | tf_op jit(solution)/shard_map/ppermute | solution.py:24
  4.0 0.7 slice-start
  4.8 26.6 %collective-permute-start.1 = (f32[32,48]{1,0:T(8,128)S(1)}, f32[32,48]{1,0:T(8,128)S(1)}, u32[]{:S(2)}, u32[]{:S(2)}) collective-permute-start(f32[32,48]{1,0:T(8,128)S(1)} %pad_maximum_fusion), channel_id=1, source_target_pairs={{0,28},{4,0},{8,4},{12,8},{16,12},{20,16},{24,20},{28,24},{1,29},{... | collective-permute-start | bytes 18440 | tf_op jit(solution)/shard_map/ppermute | solution.py:18
  10.1 0.8 copy-start.4
  11.2 19.1 %copy-start = (f32[32,384]{1,0:T(8,128)S(1)}, f32[32,384]{1,0:T(8,128)}, u32[]{:S(2)}) copy-start(f32[32,384]{1,0:T(8,128)} %param.12) | copy-start | bytes 147460
  29.6 0.7 copy-start.7
  29.6 0.7 copy-start.8
  31.6 0.8 copy-start.5
  31.6 0.8 copy-start.6
  32.6 3.1 collective-permute-start.3
  34.0 6.5 %collective-permute-start.2 = (f32[32,48]{1,0:T(8,128)S(1)}, f32[32,48]{1,0:T(8,128)S(1)}, u32[]{:S(2)}, u32[]{:S(2)}) collective-permute-start(f32[32,48]{1,0:T(8,128)S(1)} %pad_maximum_fusion.1), channel_id=1, source_target_pairs={{0,4},{4,8},{8,12},{12,16},{16,20},{20,24},{24,28},{28,0},{1,5},{5... | collective-permute-start | bytes 18440 | tf_op jit(solution)/shard_map/ppermute | solution.py:18
  40.6 0.7 copy-start.10
  40.6 0.7 copy-start.11
  42.3 21.6 %collective-permute-start.4 = (f32[2,384]{1,0:T(2,128)S(1)}, f32[2,384]{1,0:T(2,128)S(1)}, u32[]{:S(2)}, u32[]{:S(2)}) collective-permute-start(f32[2,384]{1,0:T(2,128)S(1)} %pad_maximum_fusion.20), channel_id=1, source_target_pairs={{0,1},{1,2},{2,3},{4,5},{5,6},{6,7},{8,9},{9,10},{10,11},{12,13},{... | collective-permute-start | bytes 9224 | tf_op jit(solution)/shard_map/ppermute | solution.py:24
  44.4 19.5 %collective-permute-start.5 = (f32[32,48]{1,0:T(8,128)S(1)}, f32[32,48]{1,0:T(8,128)S(1)}, u32[]{:S(2)}, u32[]{:S(2)}) collective-permute-start(f32[32,48]{1,0:T(8,128)S(1)} %pad_maximum_fusion.2), channel_id=1, source_target_pairs={{0,28},{4,0},{8,4},{12,8},{16,12},{20,16},{24,20},{28,24},{1,29},{... | collective-permute-start | bytes 18440 | tf_op jit(solution)/shard_map/ppermute | solution.py:18
  64.5 3.1 collective-permute-start.7
  66.0 6.5 %collective-permute-start.6 = (f32[32,48]{1,0:T(8,128)S(1)}, f32[32,48]{1,0:T(8,128)S(1)}, u32[]{:S(2)}, u32[]{:S(2)}) collective-permute-start(f32[32,48]{1,0:T(8,128)S(1)} %pad_maximum_fusion.3), channel_id=1, source_target_pairs={{0,4},{4,8},{8,12},{12,16},{16,20},{20,24},{24,28},{28,0},{1,5},{5... | collective-permute-start | bytes 18440 | tf_op jit(solution)/shard_map/ppermute | solution.py:18
  73.6 21.6 %collective-permute-start.8 = (f32[2,384]{1,0:T(2,128)S(1)}, f32[2,384]{1,0:T(2,128)S(1)}, u32[]{:S(2)}, u32[]{:S(2)}) collective-permute-start(f32[2,384]{1,0:T(2,128)S(1)} %pad_maximum_fusion.22), channel_id=1, source_target_pairs={{0,1},{1,2},{2,3},{4,5},{5,6},{6,7},{8,9},{9,10},{10,11},{12,13},{... | collective-permute-start | bytes 9224 | tf_op jit(solution)/shard_map/ppermute | solution.py:24
  75.7 19.5 %collective-permute-start.9 = (f32[32,48]{1,0:T(8,128)S(1)}, f32[32,48]{1,0:T(8,128)S(1)}, u32[]{:S(2)}, u32[]{:S(2)}) collective-permute-start(f32[32,48]{1,0:T(8,128)S(1)} %pad_maximum_fusion.4), channel_id=1, source_target_pairs={{0,28},{4,0},{8,4},{12,8},{16,12},{20,16},{24,20},{28,24},{1,29},{... | collective-permute-start | bytes 18440 | tf_op jit(solution)/shard_map/ppermute | solution.py:18
  95.8 3.1 collective-permute-start.11
  97.2 6.5 %collective-permute-start.10 = (f32[32,48]{1,0:T(8,128)S(1)}, f32[32,48]{1,0:T(8,128)S(1)}, u32[]{:S(2)}, u32[]{:S(2)}) collective-permute-start(f32[32,48]{1,0:T(8,128)S(1)} %pad_maximum_fusion.5), channel_id=1, source_target_pairs={{0,4},{4,8},{8,12},{12,16},{16,20},{20,24},{24,28},{28,0},{1,5},{5... | collective-permute-start | bytes 18440 | tf_op jit(solution)/shard_map/ppermute | solution.py:18
  104.8 21.6 %collective-permute-start.12 = (f32[2,384]{1,0:T(2,128)S(1)}, f32[2,384]{1,0:T(2,128)S(1)}, u32[]{:S(2)}, u32[]{:S(2)}) collective-permute-start(f32[2,384]{1,0:T(2,128)S(1)} %pad_maximum_fusion.24), channel_id=1, source_target_pairs={{0,1},{1,2},{2,3},{4,5},{5,6},{6,7},{8,9},{9,10},{10,11},{12,13},{... | collective-permute-start | bytes 9224 | tf_op jit(solution)/shard_map/ppermute | solution.py:24
  106.9 19.5 %collective-permute-start.13 = (f32[32,48]{1,0:T(8,128)S(1)}, f32[32,48]{1,0:T(8,128)S(1)}, u32[]{:S(2)}, u32[]{:S(2)}) collective-permute-start(f32[32,48]{1,0:T(8,128)S(1)} %pad_maximum_fusion.6), channel_id=1, source_target_pairs={{0,28},{4,0},{8,4},{12,8},{16,12},{20,16},{24,20},{28,24},{1,29},{... | collective-permute-start | bytes 18440 | tf_op jit(solution)/shard_map/ppermute | solution.py:18
  127.0 3.1 collective-permute-start.15
  128.5 6.5 %collective-permute-start.14 = (f32[32,48]{1,0:T(8,128)S(1)}, f32[32,48]{1,0:T(8,128)S(1)}, u32[]{:S(2)}, u32[]{:S(2)}) collective-permute-start(f32[32,48]{1,0:T(8,128)S(1)} %pad_maximum_fusion.7), channel_id=1, source_target_pairs={{0,4},{4,8},{8,12},{12,16},{16,20},{20,24},{24,28},{28,0},{1,5},{5... | collective-permute-start | bytes 18440 | tf_op jit(solution)/shard_map/ppermute | solution.py:18
  136.1 21.6 %collective-permute-start.16 = (f32[2,384]{1,0:T(2,128)S(1)}, f32[2,384]{1,0:T(2,128)S(1)}, u32[]{:S(2)}, u32[]{:S(2)}) collective-permute-start(f32[2,384]{1,0:T(2,128)S(1)} %pad_maximum_fusion.26), channel_id=1, source_target_pairs={{0,1},{1,2},{2,3},{4,5},{5,6},{6,7},{8,9},{9,10},{10,11},{12,13},{... | collective-permute-start | bytes 9224 | tf_op jit(solution)/shard_map/ppermute | solution.py:24
  138.2 19.5 %collective-permute-start.17 = (f32[32,48]{1,0:T(8,128)S(1)}, f32[32,48]{1,0:T(8,128)S(1)}, u32[]{:S(2)}, u32[]{:S(2)}) collective-permute-start(f32[32,48]{1,0:T(8,128)S(1)} %pad_maximum_fusion.8), channel_id=1, source_target_pairs={{0,28},{4,0},{8,4},{12,8},{16,12},{20,16},{24,20},{28,24},{1,29},{... | collective-permute-start | bytes 18440 | tf_op jit(solution)/shard_map/ppermute | solution.py:18
  158.3 3.1 collective-permute-start.19
  159.8 6.5 %collective-permute-start.18 = (f32[32,48]{1,0:T(8,128)S(1)}, f32[32,48]{1,0:T(8,128)S(1)}, u32[]{:S(2)}, u32[]{:S(2)}) collective-permute-start(f32[32,48]{1,0:T(8,128)S(1)} %pad_maximum_fusion.9), channel_id=1, source_target_pairs={{0,4},{4,8},{8,12},{12,16},{16,20},{20,24},{24,28},{28,0},{1,5},{5... | collective-permute-start | bytes 18440 | tf_op jit(solution)/shard_map/ppermute | solution.py:18
  167.4 21.6 %collective-permute-start.20 = (f32[2,384]{1,0:T(2,128)S(1)}, f32[2,384]{1,0:T(2,128)S(1)}, u32[]{:S(2)}, u32[]{:S(2)}) collective-permute-start(f32[2,384]{1,0:T(2,128)S(1)} %pad_maximum_fusion.28), channel_id=1, source_target_pairs={{0,1},{1,2},{2,3},{4,5},{5,6},{6,7},{8,9},{9,10},{10,11},{12,13},{... | collective-permute-start | bytes 9224 | tf_op jit(solution)/shard_map/ppermute | solution.py:24
  169.5 19.5 %collective-permute-start.21 = (f32[32,48]{1,0:T(8,128)S(1)}, f32[32,48]{1,0:T(8,128)S(1)}, u32[]{:S(2)}, u32[]{:S(2)}) collective-permute-start(f32[32,48]{1,0:T(8,128)S(1)} %pad_maximum_fusion.10), channel_id=1, source_target_pairs={{0,28},{4,0},{8,4},{12,8},{16,12},{20,16},{24,20},{28,24},{1,29},{... | collective-permute-start | bytes 18440 | tf_op jit(solution)/shard_map/ppermute | solution.py:18
  189.6 3.1 collective-permute-start.23
  191.1 6.5 %collective-permute-start.22 = (f32[32,48]{1,0:T(8,128)S(1)}, f32[32,48]{1,0:T(8,128)S(1)}, u32[]{:S(2)}, u32[]{:S(2)}) collective-permute-start(f32[32,48]{1,0:T(8,128)S(1)} %pad_maximum_fusion.11), channel_id=1, source_target_pairs={{0,4},{4,8},{8,12},{12,16},{16,20},{20,24},{24,28},{28,0},{1,5},{5... | collective-permute-start | bytes 18440 | tf_op jit(solution)/shard_map/ppermute | solution.py:18
  198.7 21.6 %collective-permute-start.24 = (f32[2,384]{1,0:T(2,128)S(1)}, f32[2,384]{1,0:T(2,128)S(1)}, u32[]{:S(2)}, u32[]{:S(2)}) collective-permute-start(f32[2,384]{1,0:T(2,128)S(1)} %pad_maximum_fusion.30), channel_id=1, source_target_pairs={{0,1},{1,2},{2,3},{4,5},{5,6},{6,7},{8,9},{9,10},{10,11},{12,13},{... | collective-permute-start | bytes 9224 | tf_op jit(solution)/shard_map/ppermute | solution.py:24
  200.8 19.5 %collective-permute-start.25 = (f32[32,48]{1,0:T(8,128)S(1)}, f32[32,48]{1,0:T(8,128)S(1)}, u32[]{:S(2)}, u32[]{:S(2)}) collective-permute-start(f32[32,48]{1,0:T(8,128)S(1)} %pad_maximum_fusion.12), channel_id=1, source_target_pairs={{0,28},{4,0},{8,4},{12,8},{16,12},{20,16},{24,20},{28,24},{1,29},{... | collective-permute-start | bytes 18440 | tf_op jit(solution)/shard_map/ppermute | solution.py:18
  220.9 3.4 %collective-permute-start.27 = (f32[2,384]{1,0:T(2,128)S(1)}, f32[2,384]{1,0:T(2,128)S(1)}, u32[]{:S(2)}, u32[]{:S(2)}) collective-permute-start(f32[2,384]{1,0:T(2,128)S(1)} %pad_maximum_fusion.31), channel_id=1, source_target_pairs={{1,0},{2,1},{3,2},{5,4},{6,5},{7,6},{9,8},{10,9},{11,10},{13,12},{... | collective-permute-start | bytes 9224 | tf_op jit(solution)/shard_map/ppermute | solution.py:24
  222.3 6.5 %collective-permute-start.26 = (f32[32,48]{1,0:T(8,128)S(1)}, f32[32,48]{1,0:T(8,128)S(1)}, u32[]{:S(2)}, u32[]{:S(2)}) collective-permute-start(f32[32,48]{1,0:T(8,128)S(1)} %pad_maximum_fusion.13), channel_id=1, source_target_pairs={{0,4},{4,8},{8,12},{12,16},{16,20},{20,24},{24,28},{28,0},{1,5},{5... | collective-permute-start | bytes 18440 | tf_op jit(solution)/shard_map/ppermute | solution.py:18
  229.9 21.9 %collective-permute-start.28 = (f32[2,384]{1,0:T(2,128)S(1)}, f32[2,384]{1,0:T(2,128)S(1)}, u32[]{:S(2)}, u32[]{:S(2)}) collective-permute-start(f32[2,384]{1,0:T(2,128)S(1)} %pad_maximum_fusion.32), channel_id=1, source_target_pairs={{0,1},{1,2},{2,3},{4,5},{5,6},{6,7},{8,9},{9,10},{10,11},{12,13},{... | collective-permute-start | bytes 9224 | tf_op jit(solution)/shard_map/ppermute | solution.py:24
  232.2 19.7 %collective-permute-start.29 = (f32[32,48]{1,0:T(8,128)S(1)}, f32[32,48]{1,0:T(8,128)S(1)}, u32[]{:S(2)}, u32[]{:S(2)}) collective-permute-start(f32[32,48]{1,0:T(8,128)S(1)} %pad_maximum_fusion.14), channel_id=1, source_target_pairs={{0,28},{4,0},{8,4},{12,8},{16,12},{20,16},{24,20},{28,24},{1,29},{... | collective-permute-start | bytes 18440 | tf_op jit(solution)/shard_map/ppermute | solution.py:18
  252.5 3.7 %collective-permute-start.31 = (f32[2,384]{1,0:T(2,128)S(1)}, f32[2,384]{1,0:T(2,128)S(1)}, u32[]{:S(2)}, u32[]{:S(2)}) collective-permute-start(f32[2,384]{1,0:T(2,128)S(1)} %pad_maximum_fusion.33), channel_id=1, source_target_pairs={{1,0},{2,1},{3,2},{5,4},{6,5},{7,6},{9,8},{10,9},{11,10},{13,12},{... | collective-permute-start | bytes 9224 | tf_op jit(solution)/shard_map/ppermute | solution.py:24
  253.9 6.5 %collective-permute-start.30 = (f32[32,48]{1,0:T(8,128)S(1)}, f32[32,48]{1,0:T(8,128)S(1)}, u32[]{:S(2)}, u32[]{:S(2)}) collective-permute-start(f32[32,48]{1,0:T(8,128)S(1)} %pad_maximum_fusion.15), channel_id=1, source_target_pairs={{0,4},{4,8},{8,12},{12,16},{16,20},{20,24},{24,28},{28,0},{1,5},{5... | collective-permute-start | bytes 18440 | tf_op jit(solution)/shard_map/ppermute | solution.py:18
  261.4 42.7 %collective-permute-start.32 = (f32[2,384]{1,0:T(2,128)S(1)}, f32[2,384]{1,0:T(2,128)S(1)}, u32[]{:S(2)}, u32[]{:S(2)}) collective-permute-start(f32[2,384]{1,0:T(2,128)S(1)} %pad_maximum_fusion.34), channel_id=1, source_target_pairs={{0,1},{1,2},{2,3},{4,5},{5,6},{6,7},{8,9},{9,10},{10,11},{12,13},{... | collective-permute-start | bytes 9224 | tf_op jit(solution)/shard_map/ppermute | solution.py:24
  264.1 40.1 %collective-permute-start.33 = (f32[32,48]{1,0:T(8,128)S(1)}, f32[32,48]{1,0:T(8,128)S(1)}, u32[]{:S(2)}, u32[]{:S(2)}) collective-permute-start(f32[32,48]{1,0:T(8,128)S(1)} %pad_maximum_fusion.16), channel_id=1, source_target_pairs={{0,28},{4,0},{8,4},{12,8},{16,12},{20,16},{24,20},{28,24},{1,29},{... | collective-permute-start | bytes 18440 | tf_op jit(solution)/shard_map/ppermute | solution.py:18
  304.4 9.2 %copy-start.1 = (f32[32,384]{1,0:T(8,128)}, f32[32,384]{1,0:T(8,128)S(1)}, u32[]{:S(2)}) copy-start(f32[32,384]{1,0:T(8,128)S(1)} %fusion.351) | copy-start | bytes 147460
  304.5 9.0 %copy-start.2 = (f32[32,384]{1,0:T(8,128)}, f32[32,384]{1,0:T(8,128)S(1)}, u32[]{:S(2)}) copy-start(f32[32,384]{1,0:T(8,128)S(1)} %get-tuple-element.34) | copy-start | bytes 147460
  304.6 9.0 %copy-start.3 = (f32[32,384]{1,0:T(8,128)}, f32[32,384]{1,0:T(8,128)S(1)}, u32[]{:S(2)}) copy-start(f32[32,384]{1,0:T(8,128)S(1)} %get-tuple-element.35) | copy-start | bytes 147460
  304.7 3.1 collective-permute-start.35
  306.1 6.5 %collective-permute-start.34 = (f32[32,48]{1,0:T(8,128)S(1)}, f32[32,48]{1,0:T(8,128)S(1)}, u32[]{:S(2)}, u32[]{:S(2)}) collective-permute-start(f32[32,48]{1,0:T(8,128)S(1)} %pad_maximum_fusion.17), channel_id=1, source_target_pairs={{0,4},{4,8},{8,12},{12,16},{16,20},{20,24},{24,28},{28,0},{1,5},{5... | collective-permute-start | bytes 18440 | tf_op jit(solution)/shard_map/ppermute | solution.py:18
  (1 other events, 0.7 us)
where the time goes:
time: 318 us; the launch traced here: 314 us
  blocking collectives  191 us (60%)
  waiting for transfers between devices  56.3 us (18%)
  starting transfers between devices  38.4 us (12%)
  local copies, waits for them, and re-layouts  15.5 us (5%)
  other arithmetic  7.34 us (2%)
  matrix products  3.48 us (1%)
    psum x9, blocking collectives, body(): cap_means = lax.psum(cap_rows, 'lon') / lon_count  191 us
    ppermute x18, waiting for transfers between devices, shifted_2(): return lax.ppermute(x, axis, [(i, (i + by) % size) for i in range(size)])  43.2 us
    ppermute x18, starting transfers between devices, shifted_3(): lax.ppermute(value, axis, [(source, source + steps) for source in range(i...  30.8 us
    ppermute x18, waiting for transfers between devices, shifted_3(): lax.ppermute(value, axis, [(source, source + steps) for source in range(i...  13.2 us
    ppermute x18, starting transfers between devices, shifted_2(): return lax.ppermute(x, axis, [(i, (i + by) % size) for i in range(size)])  7.55 us
  transfers between devices with their start and end apart: 36, of which 17 were waited for; matrix products, arithmetic and copies ran while one was open for 2% of the time, Pallas kernels for 0%

commit v1 on v0

v1 whole, which is shorter than its diff:
```python
import functools
import math

import jax
import jax.numpy as jnp
import numpy as np
from jax import lax
from jax.experimental import pallas as pl
from jax.experimental.pallas import tpu as pltpu
from jax.sharding import PartitionSpec as P

CHANNEL = 3
STEPS = 9
RADIUS_CELLS = 1529.0
COURANT = 0.9

HALO_ROWS = 8
HALO_LANES = 128
PAD = 8
FIRST = 5
MESH = pl.DeviceIdType.MESH
DIRECTIONS = [(a, b) for a in (-1, 0, 1) for b in (-1, 0, 1) if (a, b) != (0, 0)]
EN, EE, EU, HN, HE, HR = range(6)
(C_AS, C_BE, C_CN, C_DU, C_DT, C_GC, C_IC, C_JN, C_KL, C_LY) = range(10)
C_KEEP = 10


def time_step(lat_count, lon_count):
    lon_angle = 2.0 * math.pi / lon_count
    lat_angle = math.pi / lat_count
    narrowest = RADIUS_CELLS * lon_angle * math.sin(lat_angle)
    lat_length = RADIUS_CELLS * lat_angle
    return COURANT / math.sqrt(1.0 / narrowest**2 + 1.0 / lat_length**2 + 1.0)


def row_table(lat_count, lon_count):
    f = np.float32
    lon_angle = 2.0 * math.pi / lon_count
    lat_angle = math.pi / lat_count
    dt = time_step(lat_count, lon_count)
    ly = RADIUS_CELLS * math.pi / lat_count
    row = np.arange(lat_count)
    centre = f(-0.5 * math.pi) + (row.astype(f) + f(0.5)) * f(lat_angle)
    north = centre + f(0.5 * lat_angle)
    south = centre - f(0.5 * lat_angle)
    following = centre + f(lat_angle)
    pole = row == lat_count - 1
    scale = RADIUS_CELLS * lon_angle
    band = 2.0 * RADIUS_CELLS * scale * math.sin(0.5 * lat_angle)
    lc = f(scale) * np.cos(centre)
    ln = f(scale) * np.cos(following)
    le = np.where(pole, f(0), f(scale) * np.cos(north))
    ls = np.where(row == 0, f(0), f(scale) * np.cos(south))
    ls[-1] = le[-2]
    ac = f(band) * np.cos(centre)
    ae = np.where(pole, f(1), f(band) * np.cos(north))
    se = np.where(pole, f(1), le)
    keep = np.where(pole, f(0), f(1))
    table = np.zeros((lat_count + 2 * HALO_ROWS, 128), f)
    inner = table[HALO_ROWS:-HALO_ROWS]
    inner[:, C_AS] = dt * ls / ac
    inner[:, C_BE] = dt * le / ac
    inner[:, C_CN] = dt * ly / ac
    inner[:, C_DU] = keep * dt / se
    inner[:, C_DT] = keep * dt
    inner[:, C_GC] = 1.0 / lc
    inner[:, C_IC] = keep * lc / ae
    inner[:, C_JN] = keep * ln / ae
    inner[:, C_KL] = keep * ly / ae
    inner[:, C_LY] = keep / ly
    inner[:, C_KEEP] = keep
    return table


def turn(x, by):
    return pltpu.roll(x, by % x.shape[1], 1)


def div24(x):
    return lax.shift_right_logical(x * 2731, 16)


def kernel(
    dims,
    en, ee, eu, hn, he, hr, sigma, f_lat, f_lon, f_step, f_amp, table,
    o_en, o_ee, o_eu, o_hn, o_he, o_hr, o_zon,
    ext_a, ext_b, coef, lanes, src, small, sums_out, sums_in, zon_cap, zon_out, strip,
    send_a, recv_a, send_b, recv_b, send_s, recv_s, send_z, recv_z,
):
    n_lat, n_lon, layers, dt, ly = dims
    rows, width = en.shape
    wide = width + 2 * HALO_LANES
    tall = rows + 2 * HALO_ROWS
    groups = tall // 8
    vregs = wide // 128
    lat, lon = lax.axis_index("lat"), lax.axis_index("lon")
    own_r = pl.ds(PAD + HALO_ROWS, rows)
    own_c = pl.ds(HALO_LANES, width)

    def at(a, b):
        row = jnp.clip(lat + a, 0, n_lat - 1) if a else lat
        return {"lat": row, "lon": lax.rem(lon + b + n_lon, n_lon)}

    def there(a):
        return lat + a >= 0 if a < 0 else lat + a < n_lat

    def guarded(a, fn):
        if a == 0:
            fn()
        else:
            pl.when(there(a))(fn)

    barrier = pltpu.get_barrier_semaphore()

    def greet(a, b):
        pl.semaphore_signal(barrier, inc=1, device_id=at(a, b), device_id_type=MESH)

    for k in range(1, n_lon):
        greet(0, k)
    for a in (-1, 1):
        def both(a=a):
            for b in (-1, 0, 1):
                greet(a, b)
        pl.when(there(a))(both)

    keep = table[pl.ds(lat * rows + HALO_ROWS, rows), C_KEEP:C_KEEP + 1]
    keep = jnp.broadcast_to(keep, (rows, width))
    start = [en[...], keep * ee[...], keep * eu[...], keep * hn[...], he[...], hr[...]]
    low = PAD + HALO_ROWS
    for ext in (ext_a, ext_b):
        edge = jnp.zeros((6, 8, wide), jnp.float32)
        ext[:, 0:PAD, :] = edge
        ext[:, low + rows + 8:, :] = edge
        for a, first_row in ((-1, PAD), (1, low + rows)):
            def clear(ext=ext, first_row=first_row):
                ext[:, first_row:first_row + 8, :] = jnp.zeros((6, 8, wide), jnp.float32)
            pl.when(jnp.logical_not(there(a)))(clear)
    for f in range(6):
        ext_a[f, own_r, own_c] = start[f]

    def fold(x):
        for by in (width // 2, width // 4, width // 8, width // 16):
            x = x + turn(x, by)
        return x[:, :128] * (1.0 / (n_lon * (width // layers)))

    lane = lax.broadcasted_iota(jnp.int32, (rows, 128), 1)
    sums_out[...] = jnp.where(
        lane < layers,
        fold(start[EE]),
        jnp.where(lane < 2 * layers, fold(start[HN]), fold(start[HR])),
    )

    greeted = (n_lon - 1) + 3 * (lat > 0).astype(jnp.int32) + 3 * (lat < n_lat - 1).astype(jnp.int32)
    pl.semaphore_wait(barrier, greeted)

    def strip_copy(src_ref, dst_ref, sends, recvs, i):
        a, b = DIRECTIONS[i]
        def part(first, size, halo, d, side):
            if d == 0:
                return pl.ds(first, size)
            if side == 0:
                return pl.ds(first + size - halo, halo) if d > 0 else pl.ds(first, halo)
            return pl.ds(first - halo, halo) if d > 0 else pl.ds(first + size, halo)
        def cut(side):
            return (
                slice(None),
                part(PAD + HALO_ROWS, rows, HALO_ROWS, a, side),
                part(HALO_LANES, width, HALO_LANES, b, side),
            )
        return pltpu.make_async_remote_copy(
            src_ref=src_ref.at[cut(0)],
            dst_ref=dst_ref.at[cut(1)],
            send_sem=sends.at[i],
            recv_sem=recvs.at[i],
            device_id=at(a, b),
            device_id_type=MESH,
        )

    def start_all(*args):
        for i, (a, b) in enumerate(DIRECTIONS):
            guarded(a, lambda i=i: strip_copy(*args, i).start())

    def wait_sends(*args):
        for i, (a, b) in enumerate(DIRECTIONS):
            guarded(a, lambda i=i: strip_copy(*args, i).wait_send())

    def wait_recvs(*args):
        for i, (a, b) in enumerate(DIRECTIONS):
            guarded(-a, lambda i=i: strip_copy(*args, i).wait_recv())

    first = (ext_a, ext_a, send_a, recv_a)
    second = (ext_a, ext_b, send_b, recv_b)

    def sum_copy(k):
        return pltpu.make_async_remote_copy(
            src_ref=sums_out,
            dst_ref=sums_in.at[k],
            send_sem=send_s.at[k],
            recv_sem=recv_s.at[k],
            device_id=at(0, k),
            device_id_type=MESH,
        )

    start_all(*first)
    for k in range(1, n_lon):
        sum_copy(k).start()

    rows_tab = table[pl.ds(lat * rows, tall), :]
    for c in range(10):
        coef[c] = jnp.broadcast_to(rows_tab[:, c:c + 1], (tall, 128))
    small[...] = jnp.zeros((8, 128), jnp.float32)
    small[0:1, 0:layers] = sigma[...]
    one = jnp.broadcast_to(small[0:1, :], (8, 128))
    pair = one + turn(one, 24)
    sig = pair + turn(pair, 48) + turn(one, 96)
    half = 0.5 * dt * sig
    dec = (1.0 - half) / (1.0 + half)
    drv = dt / (1.0 + half)
    lane8 = lax.broadcasted_iota(jnp.int32, (8, 128), 1)

    def spread(x):
        out = []
        for v in range(vregs):
            off = (8 * v - 8) % 24
            out.append(jnp.where(lane8 < 96, turn(x, -off), turn(x, 24 - off)))
        return jnp.concatenate(out, axis=1)

    at_lane = lax.broadcasted_iota(jnp.int32, (8, wide), 1) + 16
    layer = at_lane - 24 * div24(at_lane)
    lanes[0] = spread(dec)
    lanes[1] = spread(drv)
    lanes[2] = jnp.where(layer < CHANNEL, lanes[1], 0.0)
    lanes[3] = jnp.where(layer == layers - 1, 0.0, 1.0)
    lanes[4] = jnp.where(layer == 0, 0.0, 1.0)

    strokes = f_lat.shape[1]
    place = lax.broadcasted_iota(jnp.int32, (wide, strokes), 0) + 16
    cell = div24(place) - 6 + lon * (width // layers)
    total_lon = n_lon * (width // layers)
    cell = jnp.where(cell < 0, cell + total_lon, cell)
    cell = jnp.where(cell >= total_lon, cell - total_lon, cell)
    cells = (cell == f_lon[...]).astype(jnp.float32).astype(jnp.bfloat16)
    row_no = lax.broadcasted_iota(jnp.int32, (tall, strokes), 0) + (lat * rows - HALO_ROWS)
    in_row = jnp.where(row_no == f_lat[...], jnp.broadcast_to(f_amp[...], (tall, strokes)), 0.0)
    def sources(s, carry):
        amps = jnp.where(f_step[...] == s, in_row, 0.0)
        total = None
        for _ in range(3):
            part = amps.astype(jnp.bfloat16)
            amps = amps - part.astype(jnp.float32)
            term = lax.dot_general(
                part, cells, (((1,), (1,)), ((), ())), preferred_element_type=jnp.float32
            )
            total = term if total is None else total + term
        src[pl.ds(pl.multiple_of(s * tall, 8), tall), :] = total
        return carry
    lax.fori_loop(0, STEPS, sources, 0)

    for k in range(1, n_lon):
        sum_copy(k).wait()
    mean = sums_out[...]
    for k in range(1, n_lon):
        mean = mean + sums_in[k]
    strip[own_r, :] = mean
    strip[0:low, :] = jnp.zeros((low, 128), jnp.float32)

    def zone_copy(a):
        i = 0 if a < 0 else 1
        return pltpu.make_async_remote_copy(
            src_ref=strip.at[pl.ds(low, 8) if a < 0 else pl.ds(low + rows - 8, 8), :],
            dst_ref=sums_in.at[0, pl.ds(8, 8) if a < 0 else pl.ds(0, 8), :],
            send_sem=send_z.at[i],
            recv_sem=recv_z.at[i],
            device_id=at(a, 0),
            device_id_type=MESH,
        )

    for a in (-1, 1):
        guarded(a, lambda a=a: zone_copy(a).start())

    def unpack(x):
        out = []
        lane_no = lax.broadcasted_iota(jnp.int32, x.shape, 1)
        for f in range(3):
            y = jnp.where(lane_no < layers, turn(x, -layers * f), 0.0)
            p = y + turn(y, 24)
            out.append(p + turn(p, 48) + turn(y, 96))
        return out

    zero_low = jnp.zeros((3, low, 128), jnp.float32)
    zon_cap[:, 0:low, :] = zero_low
    zon_cap[:, low + rows:, :] = zero_low
    zon_out[:, 0:low, :] = zero_low
    zon_out[:, low + rows:, :] = zero_low
    for f, z in enumerate(unpack(mean)):
        zon_cap[f, own_r, :] = z
        zon_out[f, own_r, :] = z

    z_dec, z_drv, z_top, z_bot = [lanes.at[i, :, 128:256] for i in (0, 1, 3, 4)]

    def zonal_step(zon, span):
        for g in span:
            lo, r = PAD + 8 * g, 8 * g
            east = zon[0, lo:lo + 8, :]
            zon[2, lo:lo + 8, :] = (
                zon[2, lo:lo + 8, :]
                - coef[C_AS, r:r + 8] * zon[0, lo - 1:lo + 7, :]
                + coef[C_BE, r:r + 8] * east
            )
            zon[1, lo:lo + 8, :] = zon[1, lo:lo + 8, :] - coef[C_DT, r:r + 8] * (
                z_top[...] * turn(east, -1) - east
            )
        for g in span:
            lo, r = PAD + 8 * g, 8 * g
            up, north = zon[2, lo:lo + 8, :], zon[1, lo:lo + 8, :]
            zon[0, lo:lo + 8, :] = z_dec[...] * zon[0, lo:lo + 8, :] + z_drv[...] * (
                coef[C_LY, r:r + 8] * (zon[2, lo + 1:lo + 9, :] - up)
                - (north - z_bot[...] * turn(north, 1))
            )

    def rowc(c, g):
        return jnp.concatenate([coef[c, 8 * g:8 * g + 8]] * vregs, axis=1)

    def step(ext, s):
        zonal_step(zon_cap, range(1, groups - 1))
        for g in range(groups):
            lo = PAD + 8 * g
            here = slice(lo, lo + 8)
            south = slice(lo - 1, lo + 7)
            top = lanes[3]
            e_n, e_e, e_u = ext[EN, here], ext[EE, here], ext[EU, here]
            up = (
                ext[HR, here]
                - rowc(C_AS, g) * ext[EE, south]
                + rowc(C_BE, g) * e_e
                - rowc(C_CN, g) * (turn(e_n, -layers) - e_n)
            )
            if g in (1, groups - 2):
                row = lax.broadcasted_iota(jnp.int32, (8, wide), 0) + (lat * rows - HALO_ROWS + 8 * g)
                pole = 0 if g == 1 else n_lat * rows - 1
                up = jnp.where(row == pole, spread(zon_cap[2, here]), up)
            ext[HR, here] = up
            ext[HN, here] = (
                ext[HN, here]
                - rowc(C_DU, g) * (e_u - turn(e_u, -layers))
                - rowc(C_DT, g) * (top * turn(e_e, -1) - e_e)
            )
            ext[HE, here] = (
                ext[HE, here]
                - (dt / ly) * (e_u - ext[EU, south])
                + dt * (top * turn(e_n, -1) - e_n)
            )
        for g in range(groups):
            lo = PAD + 8 * g
            here = slice(lo, lo + 8)
            north = slice(lo + 1, lo + 9)
            decay, drive, channel, bot = lanes[0], lanes[1], lanes[2], lanes[4]
            h_n, h_e, h_r = ext[HN, here], ext[HE, here], ext[HR, here]
            ext[EN, here] = decay * ext[EN, here] + drive * (
                h_e - bot * turn(h_e, 1) - rowc(C_GC, g) * (h_r - turn(h_r, layers))
            )
            ext[EE, here] = decay * ext[EE, here] + drive * (
                rowc(C_LY, g) * (ext[HR, north] - h_r) - (h_n - bot * turn(h_n, 1))
            )
            ext[EU, here] = (
                decay * ext[EU, here]
                + drive
                * (
                    rowc(C_IC, g) * h_e
                    - rowc(C_JN, g) * ext[HE, north]
                    + rowc(C_KL, g) * (h_n - turn(h_n, layers))
                )
                + channel * src[pl.ds(pl.multiple_of(s * tall + 8 * g, 8), 8), :]
            )

    def steps(ext, begin, end):
        def one_step(s, carry):
            step(ext, s)
            return carry
        lax.fori_loop(begin, end, one_step, 0)

    wait_recvs(*first)
    wait_sends(*first)
    steps(ext_a, 0, FIRST)
    start_all(*second)
    ext_b[:, own_r, own_c] = ext_a[:, own_r, own_c]

    for a in (-1, 1):
        def take(a=a):
            zone_copy(a).wait_recv()
            side = unpack(sums_in[0, 0:8, :] if a > 0 else sums_in[0, 8:16, :])
            for f in range(3):
                if a > 0:
                    zon_out[f, PAD:low, :] = side[f]
                else:
                    zon_out[f, low + rows:low + rows + 8, :] = side[f]
        guarded(-a, take)
        guarded(a, lambda a=a: zone_copy(a).wait_send())

    def record(s, carry):
        o_zon[s, 0] = zon_out[0, own_r, 0:layers]
        o_zon[s, 1] = zon_out[2, own_r, 0:layers]
        zonal_step(zon_out, range(groups))
        return carry
    lax.fori_loop(0, STEPS, record, 0)

    wait_recvs(*second)
    steps(ext_b, FIRST, STEPS)
    for f, out in ((EN, o_en), (EE, o_ee), (EU, o_eu), (HN, o_hn), (HE, o_he), (HR, o_hr)):
        out[...] = ext_b[f, own_r, own_c]
    wait_sends(*second)


def body(
    efield_north,
    efield_east,
    efield_up,
    hfield_north,
    hfield_east,
    hfield_up,
    sigma_profile,
    flash_lat,
    flash_lon,
    flash_step,
    flash_amp,
):
    rows, width = efield_north.shape
    layers = sigma_profile.shape[0]
    n_lat, n_lon = lax.axis_size("lat"), lax.axis_size("lon")
    lat_count, lon_count = rows * n_lat, (width // layers) * n_lon
    dims = (
        n_lat,
        n_lon,
        layers,
        time_step(lat_count, lon_count),
        RADIUS_CELLS * math.pi / lat_count,
    )
    wide, tall = width + 2 * HALO_LANES, rows + 2 * HALO_ROWS
    f32 = jnp.float32
    vmem = pl.BlockSpec(memory_space=pltpu.VMEM)
    field = jax.ShapeDtypeStruct((rows, width), f32)
    dma = pltpu.SemaphoreType.DMA
    return pl.pallas_call(
        functools.partial(kernel, dims),
        out_shape=[field] * 6 + [jax.ShapeDtypeStruct((STEPS, 2, rows, layers), f32)],
        in_specs=[vmem] * 12,
        out_specs=[vmem] * 7,
        scratch_shapes=[
            pltpu.VMEM((6, tall + 2 * PAD, wide), f32),
            pltpu.VMEM((6, tall + 2 * PAD, wide), f32),
            pltpu.VMEM((10, tall, 128), f32),
            pltpu.VMEM((5, 8, wide), f32),
            pltpu.VMEM((STEPS * tall, wide), f32),
            pltpu.VMEM((8, 128), f32),
            pltpu.VMEM((rows, 128), f32),
            pltpu.VMEM((n_lon, rows, 128), f32),
            pltpu.VMEM((3, tall + 2 * PAD, 128), f32),
            pltpu.VMEM((3, tall + 2 * PAD, 128), f32),
            pltpu.VMEM((tall + 2 * PAD, 128), f32),
            dma((8,)), dma((8,)), dma((8,)), dma((8,)),
            dma((n_lon,)), dma((n_lon,)), dma((2,)), dma((2,)),
        ],
        compiler_params=pltpu.CompilerParams(
            collective_id=0, has_side_effects=True, vmem_limit_bytes=32 * 1024 * 1024
        ),
    )(
        efield_north,
        efield_east,
        efield_up,
        hfield_north,
        hfield_east,
        hfield_up,
        sigma_profile[None, :],
        flash_lat[None, :],
        flash_lon[None, :],
        flash_step[None, :],
        flash_amp[None, :],
        jnp.asarray(row_table(lat_count, lon_count)),
    )


def solution(mesh):
    fields = P("lat", "lon")
    return jax.shard_map(
        body,
        mesh=mesh,
        in_specs=(fields,) * 6 + (P(),) * 5,
        out_specs=(fields,) * 6 + (P(None, None, "lat", None),),
        check_vma=False,
    )
```

time: 318 us -> 38 us (0.12)
  blocking collectives: 191 us -> 0 us
  waiting for transfers between devices: 56.3 us -> 0 us
  starting transfers between devices: 38.4 us -> 0 us
  Pallas kernels: 0 us -> 25.9 us
  other arithmetic: 7.34 us -> 0 us
  local copies, waits for them, and re-layouts: 15.5 us -> 10.9 us
  matrix products: 3.48 us -> 0 us
    psum x9 -> x0, blocking collectives: 191 us -> none  [body(): cap_means = lax.psum(cap_rows, 'lon') / lon_count]
    ppermute x36 -> x0, waiting for transfers between devices: 56.3 us -> none  [the longest x18 43.2 us: shifted_2(): return lax.ppermute(x, axis, [(i, (i + by) % size) for i in range(size)])]
    ppermute x36 -> x0, starting transfers between devices: 38.4 us -> none  [the longest x18 30.8 us: shifted_3(): lax.ppermute(value, axis, [(source, source + steps) for source in range(i...]
    pallas_call x0 -> x1, Pallas kernels: none -> 25.9 us  [body(): pl.pallas_call(functools.partial(kernel, dims), out_shape=[field] * 6 + [...]
    slice x163 -> x0, local copies, waits for them, and re-layouts: 6.43 us -> none  [the longest x18 1.36 us: level_above(): values[:, 1:]]
    unnamed x25 -> x30, local copies, waits for them, and re-layouts: 3.81 us -> 10.1 us
    dot_general x9 -> x0, matrix products: 3.48 us -> none  [body(): lax.dot_general(weighted, lon_table, (((0,), (0,)), ((), ())), precision=...]
  transfers between devices with their start and end apart: 36 -> 0, of which waited for: 17 -> 0; matrix products, arithmetic and copies ran while one was open for 2% -> 0% of each run, Pallas kernels for 0% -> 0%
where the time goes in v1:
time: 38 us; the launch traced here: 37.5 us
  Pallas kernels  25.9 us (68%)
  local copies, waits for them, and re-layouts  10.9 us (29%)
  between operations  0.7 us (2%)
    pallas_call x1, Pallas kernels, body(): pl.pallas_call(functools.partial(kernel, dims), out_shape=[field] * 6 + [...  25.9 us
    unnamed x30, local copies, waits for them, and re-layouts  10.1 us
    pallas_call x1, local copies, waits for them, and re-layouts, body(): pl.pallas_call(functools.partial(kernel, dims), out_shape=[field] * 6 + [...  0.83 us

profile of v1, /device:TPU:0, one launch (start us, length us, event | category | flops | bytes accessed | tf_op | source)
XLA Modules:
  0.0 37.5 jit_solution(8586755292223137713)
XLA Ops:
  0.6 0.0 copy-start.10
  0.6 0.0 copy-start.11
  0.7 0.0 copy-start.7
  0.7 0.0 copy-start.8
  0.7 0.0 copy-start.9
  0.7 0.6 %copy-done.10 = s32[64]{0:T(128)S(1)} copy-done((s32[64]{0:T(128)S(1)}, s32[64]{0:T(128)}, u32[]{:S(2)}) %copy-start.10) | copy-done | bytes 280
  1.3 0.0 copy-done.11
  1.3 0.0 copy-done.7
  1.3 0.0 copy-done.8
  1.3 0.0 copy-done.9
  1.4 0.0 copy-start
  1.4 0.9 %copy-done = f32[144,128]{1,0:T(8,128)S(1)} copy-done((f32[144,128]{1,0:T(8,128)S(1)}, f32[144,128]{1,0:T(8,128)}, u32[]{:S(2)}) %copy-start) | copy-done | bytes 73752
  2.2 0.0 copy-start.1
  2.2 0.8 %copy-done.1 = f32[32,384]{1,0:T(8,128)S(1)} copy-done((f32[32,384]{1,0:T(8,128)S(1)}, f32[32,384]{1,0:T(8,128)}, u32[]{:S(2)}) %copy-start.1) | copy-done | bytes 49176
  3.0 0.0 copy-start.2
  3.0 0.8 %copy-done.2 = f32[32,384]{1,0:T(8,128)S(1)} copy-done((f32[32,384]{1,0:T(8,128)S(1)}, f32[32,384]{1,0:T(8,128)}, u32[]{:S(2)}) %copy-start.2) | copy-done | bytes 49176
  3.8 0.0 copy-start.3
  3.8 0.8 %copy-done.3 = f32[32,384]{1,0:T(8,128)S(1)} copy-done((f32[32,384]{1,0:T(8,128)S(1)}, f32[32,384]{1,0:T(8,128)}, u32[]{:S(2)}) %copy-start.3) | copy-done | bytes 49176
  4.6 0.0 copy-start.4
  4.6 0.8 %copy-done.4 = f32[32,384]{1,0:T(8,128)S(1)} copy-done((f32[32,384]{1,0:T(8,128)S(1)}, f32[32,384]{1,0:T(8,128)}, u32[]{:S(2)}) %copy-start.4) | copy-done | bytes 49176
  5.4 0.0 copy-start.5
  5.4 0.8 %copy-done.5 = f32[32,384]{1,0:T(8,128)S(1)} copy-done((f32[32,384]{1,0:T(8,128)S(1)}, f32[32,384]{1,0:T(8,128)}, u32[]{:S(2)}) %copy-start.5) | copy-done | bytes 49176
  6.2 0.0 copy-start.6
  6.2 0.8 %copy-done.6 = f32[32,384]{1,0:T(8,128)S(1)} copy-done((f32[32,384]{1,0:T(8,128)S(1)}, f32[32,384]{1,0:T(8,128)}, u32[]{:S(2)}) %copy-start.6) | copy-done | bytes 49176
  7.0 25.9 %shard_map.171 = (f32[32,384]{1,0:T(8,128)S(1)}, f32[32,384]{1,0:T(8,128)S(1)}, f32[32,384]{1,0:T(8,128)S(1)}, f32[32,384]{1,0:T(8,128)S(1)}, f32[32,384]{1,0:T(...) custom-call(f32[32,384]{1,0:T(8,128)S(1)} %copy-done.1, f32[32,384]{1,0:T(8,128)S(1)} %copy-done.2, ...), custom_call_target="tpu_custom_call" | custom-call | tf_op jit(solution)/shard_map/pallas_call | solution.py:443
  32.9 0.8 %copy.19 = f32[9,2,32,24]{2,3,1,0:T(8,128)} copy(f32[9,2,32,24]{3,2,1,0:T(8,128)S(1)} %get-tuple-element.13) | data formatting | bytes 110592 | tf_op jit(solution)/shard_map/pallas_call | solution.py:443
  33.8 0.6 %copy.26 = f32[32,384]{1,0:T(8,128)} copy(f32[32,384]{1,0:T(8,128)S(1)} %get-tuple-element.21) | data formatting | bytes 98304
  34.4 0.6 %copy.27 = f32[32,384]{1,0:T(8,128)} copy(f32[32,384]{1,0:T(8,128)S(1)} %get-tuple-element.22) | data formatting | bytes 98304
  35.0 0.6 %copy.28 = f32[32,384]{1,0:T(8,128)} copy(f32[32,384]{1,0:T(8,128)S(1)} %get-tuple-element.23) | data formatting | bytes 98304
  35.6 0.6 %copy.29 = f32[32,384]{1,0:T(8,128)} copy(f32[32,384]{1,0:T(8,128)S(1)} %get-tuple-element.24) | data formatting | bytes 98304
  36.2 0.6 %copy.30 = f32[32,384]{1,0:T(8,128)} copy(f32[32,384]{1,0:T(8,128)S(1)} %get-tuple-element.25) | data formatting | bytes 98304
  36.9 0.6 %copy.31 = f32[32,384]{1,0:T(8,128)} copy(f32[32,384]{1,0:T(8,128)S(1)} %get-tuple-element.26) | data formatting | bytes 98304
Async XLA Ops:
  0.6 0.7 %copy-start.10 = (s32[64]{0:T(128)S(1)}, s32[64]{0:T(128)}, u32[]{:S(2)}) copy-start(s32[64]{0:T(128)} %param.21) | copy-start | bytes 772
  0.6 0.7 %copy-start.11 = (f32[64]{0:T(128)S(1)}, f32[64]{0:T(128)}, u32[]{:S(2)}) copy-start(f32[64]{0:T(128)} %param.22) | copy-start | bytes 772
  0.7 0.7 %copy-start.7 = (f32[24]{0:T(128)S(1)}, f32[24]{0:T(128)}, u32[]{:S(2)}) copy-start(f32[24]{0:T(128)} %param.18) | copy-start | bytes 292
  0.7 0.7 %copy-start.8 = (s32[64]{0:T(128)S(1)}, s32[64]{0:T(128)}, u32[]{:S(2)}) copy-start(s32[64]{0:T(128)} %param.19) | copy-start | bytes 772
  0.7 0.7 %copy-start.9 = (s32[64]{0:T(128)S(1)}, s32[64]{0:T(128)}, u32[]{:S(2)}) copy-start(s32[64]{0:T(128)} %param.20) | copy-start | bytes 772
  1.4 0.9 %copy-start = (f32[144,128]{1,0:T(8,128)S(1)}, f32[144,128]{1,0:T(8,128)}, u32[]{:S(2)}) copy-start(f32[144,128]{1,0:T(8,128)} %constant.2.clone.table) | copy-start | bytes 221188
  2.2 0.8 %copy-start.1 = (f32[32,384]{1,0:T(8,128)S(1)}, f32[32,384]{1,0:T(8,128)}, u32[]{:S(2)}) copy-start(f32[32,384]{1,0:T(8,128)} %en.1) | copy-start | bytes 147460
  3.0 0.8 %copy-start.2 = (f32[32,384]{1,0:T(8,128)S(1)}, f32[32,384]{1,0:T(8,128)}, u32[]{:S(2)}) copy-start(f32[32,384]{1,0:T(8,128)} %ee.1) | copy-start | bytes 147460
  3.8 0.8 %copy-start.3 = (f32[32,384]{1,0:T(8,128)S(1)}, f32[32,384]{1,0:T(8,128)}, u32[]{:S(2)}) copy-start(f32[32,384]{1,0:T(8,128)} %eu.1) | copy-start | bytes 147460
  4.6 0.8 %copy-start.4 = (f32[32,384]{1,0:T(8,128)S(1)}, f32[32,384]{1,0:T(8,128)}, u32[]{:S(2)}) copy-start(f32[32,384]{1,0:T(8,128)} %hn.1) | copy-start | bytes 147460
  5.4 0.8 %copy-start.5 = (f32[32,384]{1,0:T(8,128)S(1)}, f32[32,384]{1,0:T(8,128)}, u32[]{:S(2)}) copy-start(f32[32,384]{1,0:T(8,128)} %he.1) | copy-start | bytes 147460
  6.2 0.8 %copy-start.6 = (f32[32,384]{1,0:T(8,128)S(1)}, f32[32,384]{1,0:T(8,128)}, u32[]{:S(2)}) copy-start(f32[32,384]{1,0:T(8,128)} %hr.1) | copy-start | bytes 147460

commit v2 on v1

--- a/solution.py
+++ b/solution.py
@@ -13,6 +13,7 @@
 STEPS = 9
 RADIUS_CELLS = 1529.0
 COURANT = 0.9
+VMEM_GRANT = 63 * 1024 * 1024
 
 HALO_ROWS = 8
 HALO_LANES = 128
@@ -82,13 +83,15 @@
 
 def kernel(
     dims,
-    en, ee, eu, hn, he, hr, sigma, f_lat, f_lon, f_step, f_amp, table,
+    en, ee, eu, hn, he, hr, h_sigma, h_lat, h_lon, h_step, h_amp, h_table,
     o_en, o_ee, o_eu, o_hn, o_he, o_hr, o_zon,
     ext_a, ext_b, coef, lanes, src, small, sums_out, sums_in, zon_cap, zon_out, strip,
-    send_a, recv_a, send_b, recv_b, send_s, recv_s, send_z, recv_z,
+    sigma, f_lat, f_lon, f_step, f_amp, table,
+    load, send_a, recv_a, send_b, recv_b, send_s, recv_s, send_z, recv_z,
 ):
     n_lat, n_lon, layers, dt, ly = dims
     rows, width = en.shape
+    strokes = h_lat.shape[1]
     wide = width + 2 * HALO_LANES
     tall = rows + 2 * HALO_ROWS
     groups = tall // 8
@@ -110,6 +113,19 @@
         else:
             pl.when(there(a))(fn)
 
+    loads = [
+        pltpu.make_async_copy(x, ext_a.at[f, own_r, own_c], load.at[f])
+        for f, x in enumerate((en, ee, eu, hn, he, hr))
+    ]
+    here_rows = h_table.at[pl.ds(pl.multiple_of(lat * rows, 8), tall), :]
+    pairs = (
+        (here_rows, table), (h_sigma, sigma), (h_lat, f_lat), (h_lon, f_lon),
+        (h_step, f_step), (h_amp, f_amp),
+    )
+    loads += [pltpu.make_async_copy(x, y, load.at[6 + i]) for i, (x, y) in enumerate(pairs)]
+    for copy in loads:
+        copy.start()
+
     barrier = pltpu.get_barrier_semaphore()
 
     def greet(a, b):
@@ -123,9 +139,6 @@
                 greet(a, b)
         pl.when(there(a))(both)
 
-    keep = table[pl.ds(lat * rows + HALO_ROWS, rows), C_KEEP:C_KEEP + 1]
-    keep = jnp.broadcast_to(keep, (rows, width))
-    start = [en[...], keep * ee[...], keep * eu[...], keep * hn[...], he[...], hr[...]]
     low = PAD + HALO_ROWS
     for ext in (ext_a, ext_b):
         edge = jnp.zeros((6, 8, wide), jnp.float32)
@@ -135,8 +148,12 @@
             def clear(ext=ext, first_row=first_row):
                 ext[:, first_row:first_row + 8, :] = jnp.zeros((6, 8, wide), jnp.float32)
             pl.when(jnp.logical_not(there(a)))(clear)
-    for f in range(6):
-        ext_a[f, own_r, own_c] = start[f]
+    for copy in loads:
+        copy.wait()
+    last = pl.ds(low + rows - 8, 8)
+    keep = jnp.broadcast_to(table[HALO_ROWS + rows - 8:HALO_ROWS + rows, C_KEEP:C_KEEP + 1], (8, width))
+    for f in (EE, EU, HN):
+        ext_a[f, last, own_c] = keep * ext_a[f, last, own_c]
 
     def fold(x):
         for by in (width // 2, width // 4, width // 8, width // 16):
@@ -146,8 +163,8 @@
     lane = lax.broadcasted_iota(jnp.int32, (rows, 128), 1)
     sums_out[...] = jnp.where(
         lane < layers,
-        fold(start[EE]),
-        jnp.where(lane < 2 * layers, fold(start[HN]), fold(start[HR])),
+        fold(ext_a[EE, own_r, own_c]),
+        jnp.where(lane < 2 * layers, fold(ext_a[HN, own_r, own_c]), fold(ext_a[HR, own_r, own_c])),
     )
 
     greeted = (n_lon - 1) + 3 * (lat > 0).astype(jnp.int32) + 3 * (lat < n_lat - 1).astype(jnp.int32)
@@ -205,7 +222,7 @@
     for k in range(1, n_lon):
         sum_copy(k).start()
 
-    rows_tab = table[pl.ds(lat * rows, tall), :]
+    rows_tab = table[...]
     for c in range(10):
         coef[c] = jnp.broadcast_to(rows_tab[:, c:c + 1], (tall, 128))
     small[...] = jnp.zeros((8, 128), jnp.float32)
@@ -233,7 +250,6 @@
     lanes[3] = jnp.where(layer == layers - 1, 0.0, 1.0)
     lanes[4] = jnp.where(layer == 0, 0.0, 1.0)
 
-    strokes = f_lat.shape[1]
     place = lax.broadcasted_iota(jnp.int32, (wide, strokes), 0) + 16
     cell = div24(place) - 6 + lon * (width // layers)
     total_lon = n_lon * (width // layers)
@@ -398,8 +414,10 @@
         guarded(a, lambda a=a: zone_copy(a).wait_send())
 
     def record(s, carry):
-        o_zon[s, 0] = zon_out[0, own_r, 0:layers]
-        o_zon[s, 1] = zon_out[2, own_r, 0:layers]
+        both = jnp.where(lane < layers, zon_out[0, own_r, :], turn(zon_out[2, own_r, :], layers))
+        both = jnp.transpose(both)
+        o_zon[s, 0] = both[0:layers]
+        o_zon[s, 1] = both[layers:2 * layers]
         zonal_step(zon_out, range(groups))
         return carry
     lax.fori_loop(0, STEPS, record, 0)
@@ -409,6 +427,18 @@
     for f, out in ((EN, o_en), (EE, o_ee), (EU, o_eu), (HN, o_hn), (HE, o_he), (HR, o_hr)):
         out[...] = ext_b[f, own_r, own_c]
     wait_sends(*second)
+
+
+def hand_over(*refs):
+    count = len(refs) // 2
+    sems = refs[-1]
+    copies = [
+        pltpu.make_async_copy(refs[i], refs[count + i], sems.at[i]) for i in range(count)
+    ]
+    for copy in copies:
+        copy.start()
+    for copy in copies:
+        copy.wait()
 
 
 def body(
@@ -440,10 +470,13 @@
     vmem = pl.BlockSpec(memory_space=pltpu.VMEM)
     field = jax.ShapeDtypeStruct((rows, width), f32)
     dma = pltpu.SemaphoreType.DMA
-    return pl.pallas_call(
+    hbm = pl.BlockSpec(memory_space=pltpu.HBM)
+    strokes = flash_lat.shape[0]
+    outs = [field] * 6 + [jax.ShapeDtypeStruct((STEPS, 2, layers, rows), f32)]
+    results = pl.pallas_call(
         functools.partial(kernel, dims),
-        out_shape=[field] * 6 + [jax.ShapeDtypeStruct((STEPS, 2, rows, layers), f32)],
-        in_specs=[vmem] * 12,
+        out_shape=outs,
+        in_specs=[hbm] * 12,
         out_specs=[vmem] * 7,
         scratch_shapes=[
             pltpu.VMEM((6, tall + 2 * PAD, wide), f32),
@@ -457,11 +490,18 @@
             pltpu.VMEM((3, tall + 2 * PAD, 128), f32),
             pltpu.VMEM((3, tall + 2 * PAD, 128), f32),
             pltpu.VMEM((tall + 2 * PAD, 128), f32),
+            pltpu.VMEM((1, layers), f32),
+            pltpu.VMEM((1, strokes), jnp.int32),
+            pltpu.VMEM((1, strokes), jnp.int32),
+            pltpu.VMEM((1, strokes), jnp.int32),
+            pltpu.VMEM((1, strokes), f32),
+            pltpu.VMEM((tall, 128), f32),
+            dma((12,)),
             dma((8,)), dma((8,)), dma((8,)), dma((8,)),
             dma((n_lon,)), dma((n_lon,)), dma((2,)), dma((2,)),
         ],
         compiler_params=pltpu.CompilerParams(
-            collective_id=0, has_side_effects=True, vmem_limit_bytes=32 * 1024 * 1024
+            collective_id=0, has_side_effects=True, vmem_limit_bytes=VMEM_GRANT
         ),
     )(
         efield_north,
@@ -477,6 +517,15 @@
         flash_amp[None, :],
         jnp.asarray(row_table(lat_count, lon_count)),
     )
+    results = pl.pallas_call(
+        hand_over,
+        out_shape=outs,
+        in_specs=[hbm] * 7,
+        out_specs=[hbm] * 7,
+        scratch_shapes=[dma((7,))],
+        compiler_params=pltpu.CompilerParams(vmem_limit_bytes=VMEM_GRANT),
+    )(*results)
+    return (*results[:6], jnp.transpose(results[6], (0, 1, 3, 2)))
 
 
 def solution(mesh):

time: 38 us -> 44.5 us (1.17)
  Pallas kernels: 25.9 us -> 43.7 us
  local copies, waits for them, and re-layouts: 10.9 us -> 0 us
    pallas_call x1 -> x2, Pallas kernels: 25.9 us -> 43.7 us  [the longest x1 26.9 us: body(): pl.pallas_call(functools.partial(kernel, dims), out_shape=outs, in_specs=...]
    unnamed x30 -> x0, local copies, waits for them, and re-layouts: 10.1 us -> none
    pallas_call x1 -> x0, local copies, waits for them, and re-layouts: 0.83 us -> none  [body(): pl.pallas_call(functools.partial(kernel, dims), out_shape=[field] * 6 + [...]
where the time goes in v2:
time: 44.5 us; the launch traced here: 44.3 us
  Pallas kernels  43.7 us (98%)
  between operations  0.64 us (1%)
    pallas_call x1, Pallas kernels, body(): pl.pallas_call(functools.partial(kernel, dims), out_shape=outs, in_specs=...  26.9 us
    pallas_call x1, Pallas kernels, body(): pl.pallas_call(hand_over, out_shape=outs, in_specs=[hbm] * 7, out_specs=[...  16.8 us

profile of v2, /device:TPU:0, one launch (start us, length us, event | category | flops | bytes accessed | tf_op | source)
XLA Modules:
  0.0 44.3 jit_solution(14056870096808019548)
XLA Ops:
  0.6 26.9 %shard_map.171 = (f32[32,384]{1,0:T(8,128)}, f32[32,384]{1,0:T(8,128)}, f32[32,384]{1,0:T(8,128)}, f32[32,384]{1,0:T(8,128)}, f32[32,384]{1,0:T(8,128)}, /*index=5*/f32[32,384]{1,0:T(8,128)}, f32[9,2,24,32]{3,2,1,0:T(8,128)}) custom-call(f32[32,384]{1,0:T(8,128)} %en.1, f32[32,384]{1,0:T(8,128)} %ee.1, f32[32,384]{1,0:T(8,128)} %eu.1, f32[32,384]{1,0:T(8,128)} %hn.1, ...), custom_call_target="tpu_custom_call" | custom-call | tf_op jit(solution)/shard_map/pallas_call | solution.py:476
  27.5 16.8 %shard_map.172 = (f32[32,384]{1,0:T(8,128)}, f32[32,384]{1,0:T(8,128)}, f32[32,384]{1,0:T(8,128)}, f32[32,384]{1,0:T(8,128)}, f32[32,384]{1,0:T(8,128)}, /*index=5*/f32[32,384]{1,0:T(8,128)}, f32[9,2,24,32]{3,2,1,0:T(8,128)}) custom-call(f32[32,384]{1,0:T(8,128)} %get-tuple-element.21.refs_0_, f32[32,384]{1,0:T(8,128)} %get-tuple-element.22.refs_1_, ...), custom_call_target="tpu_custom_call" | custom-call | tf_op jit(solution)/shard_map/pallas_call | solution.py:520

commit v3 on v2

--- a/solution.py
+++ b/solution.py
@@ -181,7 +181,7 @@
         def cut(side):
             return (
                 slice(None),
-                part(PAD + HALO_ROWS, rows, HALO_ROWS, a, side),
+                part(PAD + HALO_ROWS, rows, FIRST, a, side),
                 part(HALO_LANES, width, HALO_LANES, b, side),
             )
         return pltpu.make_async_remote_copy(
@@ -218,9 +218,9 @@
             device_id_type=MESH,
         )
 
-    start_all(*first)
     for k in range(1, n_lon):
         sum_copy(k).start()
+    start_all(*first)
 
     rows_tab = table[...]
     for c in range(10):
@@ -430,14 +430,16 @@
 
 
 def hand_over(*refs):
-    count = len(refs) // 2
-    sems = refs[-1]
-    copies = [
-        pltpu.make_async_copy(refs[i], refs[count + i], sems.at[i]) for i in range(count)
-    ]
-    for copy in copies:
+    count = len(refs) // 3
+    sources, results, held, sems = refs[:count], refs[count:2 * count], refs[2 * count:-1], refs[-1]
+    ins = [pltpu.make_async_copy(sources[i], held[i], sems.at[i]) for i in range(count)]
+    outs = [pltpu.make_async_copy(held[i], results[i], sems.at[count + i]) for i in range(count)]
+    for copy in ins:
         copy.start()
-    for copy in copies:
+    for come, go in zip(ins, outs):
+        come.wait()
+        go.start()
+    for copy in outs:
         copy.wait()
 
 
@@ -522,7 +524,7 @@
         out_shape=outs,
         in_specs=[hbm] * 7,
         out_specs=[hbm] * 7,
-        scratch_shapes=[dma((7,))],
+        scratch_shapes=[pltpu.VMEM(x.shape, x.dtype) for x in outs] + [dma((14,))],
         compiler_params=pltpu.CompilerParams(vmem_limit_bytes=VMEM_GRANT),
     )(*results)
     return (*results[:6], jnp.transpose(results[6], (0, 1, 3, 2)))

time: 44.5 us -> 28.4 us (0.64)
  Pallas kernels: 43.7 us -> 27.6 us
    pallas_call x1, Pallas kernels: 16.8 us -> 1.9 us  [body(): pl.pallas_call(hand_over, out_shape=outs, in_specs=[hbm] * 7, out_specs=[...]
    pallas_call x1, Pallas kernels: 26.9 us -> 25.7 us  [body(): pl.pallas_call(functools.partial(kernel, dims), out_shape=outs, in_specs=...]
where the time goes in v3:
time: 28.4 us; the launch traced here: 28.2 us
  Pallas kernels  27.6 us (97%)
  between operations  0.64 us (2%)
    pallas_call x1, Pallas kernels, body(): pl.pallas_call(functools.partial(kernel, dims), out_shape=outs, in_specs=...  25.7 us
    pallas_call x1, Pallas kernels, body(): pl.pallas_call(hand_over, out_shape=outs, in_specs=[hbm] * 7, out_specs=[...  1.9 us

profile of v3, /device:TPU:0, one launch (start us, length us, event | category | flops | bytes accessed | tf_op | source)
XLA Modules:
  0.0 28.2 jit_solution(16899321961323467334)
XLA Ops:
  0.6 25.7 %shard_map.171 = (f32[32,384]{1,0:T(8,128)}, f32[32,384]{1,0:T(8,128)}, f32[32,384]{1,0:T(8,128)}, f32[32,384]{1,0:T(8,128)}, f32[32,384]{1,0:T(8,128)}, /*index=5*/f32[32,384]{1,0:T(8,128)}, f32[9,2,24,32]{3,2,1,0:T(8,128)}) custom-call(f32[32,384]{1,0:T(8,128)} %en.1, f32[32,384]{1,0:T(8,128)} %ee.1, f32[32,384]{1,0:T(8,128)} %eu.1, f32[32,384]{1,0:T(8,128)} %hn.1, ...), custom_call_target="tpu_custom_call" | custom-call | tf_op jit(solution)/shard_map/pallas_call | solution.py:478
  26.3 1.9 %shard_map.172 = (f32[32,384]{1,0:T(8,128)}, f32[32,384]{1,0:T(8,128)}, f32[32,384]{1,0:T(8,128)}, f32[32,384]{1,0:T(8,128)}, f32[32,384]{1,0:T(8,128)}, /*index=5*/f32[32,384]{1,0:T(8,128)}, f32[9,2,24,32]{3,2,1,0:T(8,128)}) custom-call(f32[32,384]{1,0:T(8,128)} %get-tuple-element.21.refs_0_, f32[32,384]{1,0:T(8,128)} %get-tuple-element.22.refs_1_, ...), custom_call_target="tpu_custom_call" | custom-call | tf_op jit(solution)/shard_map/pallas_call | solution.py:522

commit v4 on v3

--- a/solution.py
+++ b/solution.py
@@ -172,6 +172,7 @@
 
     def strip_copy(src_ref, dst_ref, sends, recvs, i):
         a, b = DIRECTIONS[i]
+        depth = FIRST if dst_ref is ext_a else STEPS - FIRST
         def part(first, size, halo, d, side):
             if d == 0:
                 return pl.ds(first, size)
@@ -181,7 +182,7 @@
         def cut(side):
             return (
                 slice(None),
-                part(PAD + HALO_ROWS, rows, FIRST, a, side),
+                part(PAD + HALO_ROWS, rows, depth, a, side),
                 part(HALO_LANES, width, HALO_LANES, b, side),
             )
         return pltpu.make_async_remote_copy(
@@ -270,7 +271,7 @@
             total = term if total is None else total + term
         src[pl.ds(pl.multiple_of(s * tall, 8), tall), :] = total
         return carry
-    lax.fori_loop(0, STEPS, sources, 0)
+    lax.fori_loop(0, FIRST, sources, 0)
 
     for k in range(1, n_lon):
         sum_copy(k).wait()
@@ -401,6 +402,7 @@
     start_all(*second)
     ext_b[:, own_r, own_c] = ext_a[:, own_r, own_c]
 
+    lax.fori_loop(FIRST, STEPS, sources, 0)
     for a in (-1, 1):
         def take(a=a):
             zone_copy(a).wait_recv()

time: 28.4 us -> 28.3 us (level)
  no operation moved by 1% of the time
where the time goes in v4:
time: 28.3 us; the launch traced here: 28.1 us
  Pallas kernels  27.5 us (97%)
  between operations  0.64 us (2%)
    pallas_call x1, Pallas kernels, body(): pl.pallas_call(functools.partial(kernel, dims), out_shape=outs, in_specs=...  25.6 us
    pallas_call x1, Pallas kernels, body(): pl.pallas_call(hand_over, out_shape=outs, in_specs=[hbm] * 7, out_specs=[...  1.9 us

profile of v4, /device:TPU:0, one launch (start us, length us, event | category | flops | bytes accessed | tf_op | source)
XLA Modules:
  0.0 28.1 jit_solution(14077445371952749867)
XLA Ops:
  0.6 25.6 %shard_map.171 = (f32[32,384]{1,0:T(8,128)}, f32[32,384]{1,0:T(8,128)}, f32[32,384]{1,0:T(8,128)}, f32[32,384]{1,0:T(8,128)}, f32[32,384]{1,0:T(8,128)}, /*index=5*/f32[32,384]{1,0:T(8,128)}, f32[9,2,24,32]{3,2,1,0:T(8,128)}) custom-call(f32[32,384]{1,0:T(8,128)} %en.1, f32[32,384]{1,0:T(8,128)} %ee.1, f32[32,384]{1,0:T(8,128)} %eu.1, f32[32,384]{1,0:T(8,128)} %hn.1, ...), custom_call_target="tpu_custom_call" | custom-call | tf_op jit(solution)/shard_map/pallas_call | solution.py:480
  26.2 1.9 %shard_map.172 = (f32[32,384]{1,0:T(8,128)}, f32[32,384]{1,0:T(8,128)}, f32[32,384]{1,0:T(8,128)}, f32[32,384]{1,0:T(8,128)}, f32[32,384]{1,0:T(8,128)}, /*index=5*/f32[32,384]{1,0:T(8,128)}, f32[9,2,24,32]{3,2,1,0:T(8,128)}) custom-call(f32[32,384]{1,0:T(8,128)} %get-tuple-element.21.refs_0_, f32[32,384]{1,0:T(8,128)} %get-tuple-element.22.refs_1_, ...), custom_call_target="tpu_custom_call" | custom-call | tf_op jit(solution)/shard_map/pallas_call | solution.py:524
